TPU v7x, 32 devices: a whole 2x2x4 slice. The times are simulated.
32 devices in a mesh: pitch: 2 (over core), axial: 4 (over y, x), span: 4 (over z).
Axes of the slice: x: 2, y: 2, z: 4, core: 2. Of those that a mesh axis runs over, the one named last changes fastest.
Arguments:
- state: float32 [5, 16, 128, 512], P(None, 'pitch', 'axial', 'span'), as said below
- coeffs: float32 [2, 4, 5, 128, 512], P(None, None, None, 'axial', 'span'), may hold values from -3 to 3
- lag_shift: int32 [1], replicated, may hold values from 0 to 63
- harmonics: int32 [512], P('span'), may hold values from 1 to 4
Outputs:
- new_state: float32 [5, 16, 128, 512], P(None, 'pitch', 'axial', 'span')
Inputs may be any that keep to these rules, and one draw needn't show every extreme that they name: `state`: density lies in 0.8 to 1.25, momenta within -1.5 to 1.5, total energy within 1.6 to 3.4.
All inputs are finite; a program needn't handle non-finite values.
Results may differ from a plain program's by a relative error of at most 0.0001.
Values sent between devices are 32-bit elements; how exact they have to be, the bound alone decides.
A program may use at most 64 MiB of HBM per device.

v0:
```python
import functools
import math

import jax
import jax.numpy as jnp
from jax import lax
from jax.experimental import pallas as pl
from jax.experimental.pallas import tpu as pltpu
from jax.sharding import PartitionSpec as P

PERIOD_SAMPLES = 64
HEAT_RATIO_GAS = 1.4
STEP_RATE = 0.25
DAMPING = 0.5
EDGE = (1.0, -8.0, 28.0, -56.0)
MESH = pl.DeviceIdType.MESH


def line_root(main, side):
    root = (-main + math.sqrt(main * main - 4.0 * side * side)) / (2.0 * side)
    return root, 1.0 / (main + 2.0 * side * root)


def pick(position, values):
    chosen = jnp.float32(values[-1])
    for index in range(len(values) - 1):
        chosen = jnp.where(position == index, jnp.float32(values[index]), chosen)
    return chosen


def kernel(
    sizes,
    lag_hbm,
    harm_hbm,
    state_hbm,
    coef_hbm,
    out_ref,
    u,
    co,
    flux,
    sums,
    got_sums,
    ax_tail,
    ax_head,
    got_tail,
    got_head,
    sp_own,
    got_left,
    got_right,
    waves,
    lag_ref,
    harm_ref,
    local_sem,
    send_sem,
    recv_sem,
):
    npitch, naxial, nspan = sizes
    fields, cells, rows, _ = u.shape
    tiles = rows // 8
    harm_max = co.shape[1]
    total = cells * npitch
    diffusion = float(total * total // 64)
    r, r_scale = line_root(1.0, 0.25)
    q, q_scale = line_root(1.0 + 2.0 * diffusion, -diffusion)
    pitch, axial, span = (lax.axis_index(name) for name in ("pitch", "axial", "span"))

    state_copy = pltpu.make_async_copy(state_hbm, u, local_sem.at[0])
    coef_copy = pltpu.make_async_copy(coef_hbm, co, local_sem.at[1])
    state_copy.start()

    barrier = pltpu.get_barrier_semaphore()

    def greet(**where):
        pl.semaphore_signal(barrier, inc=1, device_id=where, device_id_type=MESH)

    has_up, has_down = axial > 0, axial < naxial - 1
    has_left, has_right = span > 0, span < nspan - 1

    @pl.when(has_up)
    def _():
        greet(axial=axial - 1)

    @pl.when(has_down)
    def _():
        greet(axial=axial + 1)

    @pl.when(has_left)
    def _():
        greet(span=span - 1)

    @pl.when(has_right)
    def _():
        greet(span=span + 1)

    for step in range(1, npitch):
        greet(pitch=lax.rem(pitch + step, npitch))
    coef_copy.start()
    small_copies = [
        pltpu.make_async_copy(lag_hbm, lag_ref, local_sem.at[2]),
        pltpu.make_async_copy(harm_hbm, harm_ref, local_sem.at[3]),
    ]
    for copy in small_copies:
        copy.start()

    row = lax.broadcasted_iota(jnp.int32, (8, 128), 0)
    lane = lax.broadcasted_iota(jnp.int32, (8, 128), 1)
    group = lane // 8
    low_rows = row < 4

    state_copy.wait()

    def pack_axial(f, carry):
        for k in range(cells // 2):
            a, b = u[f, 2 * k, rows - 8 :, :], u[f, 2 * k + 1, rows - 8 :, :]
            ax_tail[f, k] = jnp.where(low_rows, pltpu.roll(a, 4, 0), b)
            a, b = u[f, 2 * k, :8, :], u[f, 2 * k + 1, :8, :]
            ax_head[f, k] = jnp.where(low_rows, a, pltpu.roll(b, 4, 0))
        return carry

    lax.fori_loop(0, fields, pack_axial, 0, unroll=True)

    neighbours = npitch - 1
    for flag in (has_up, has_down, has_left, has_right):
        neighbours = neighbours + jnp.where(flag, 1, 0)
    pl.semaphore_wait(barrier, neighbours)

    def remote(src, dst, slot, **where):
        return pltpu.make_async_remote_copy(
            src_ref=src,
            dst_ref=dst,
            send_sem=send_sem.at[slot],
            recv_sem=recv_sem.at[slot],
            device_id=where,
            device_id_type=MESH,
        )

    down_copy = remote(ax_tail, got_tail, 0, axial=axial + 1)
    up_copy = remote(ax_head, got_head, 1, axial=axial - 1)
    right_copy = remote(sp_own, got_left, 2, span=span + 1)
    left_copy = remote(sp_own, got_right, 3, span=span - 1)

    def when(flag, action):
        @pl.when(flag)
        def _():
            action()

    def clear(ref):
        ref[...] = jnp.zeros_like(ref)

    odd = lax.rem(axial, 2) == 1
    when(jnp.logical_and(has_up, odd), up_copy.start)
    when(has_down, down_copy.start)
    when(jnp.logical_and(has_up, jnp.logical_not(odd)), up_copy.start)

    half = cells // (sp_own.shape[1])

    def pack_span(f, carry):
        for g in range(sp_own.shape[1]):
            packed = jnp.zeros((8, 128), jnp.float32)
            for k in range(16):
                tile = u[f, g * half + k // tiles, (k % tiles) * 8 : (k % tiles) * 8 + 8, :]
                packed = jnp.where(group == k, pltpu.roll(tile, (8 * k + 4) % 128, 1), packed)
            sp_own[f, g] = packed
        return carry

    lax.fori_loop(0, fields, pack_span, 0, unroll=True)
    when(has_right, right_copy.start)
    when(has_left, left_copy.start)

    def flux_tile(t, carry):
        at = pl.ds(pl.multiple_of(t * 8, 8), 8)
        parts = [None] * 4
        for i in range(cells):
            cell = [u[f, i, at, :] for f in range(fields)]
            inverse = 1.0 / cell[0]
            speed = cell[2] * inverse
            kinetic = 0.5 * (cell[1] * cell[1] + cell[2] * cell[2] + cell[3] * cell[3]) * inverse
            pressure = (HEAT_RATIO_GAS - 1.0) * (cell[4] - kinetic)
            values = [
                cell[2],
                cell[1] * speed,
                cell[2] * speed + pressure,
                cell[3] * speed,
                (cell[4] + pressure) * speed,
            ]
            for f in range(fields):
                flux[f, i, at, :] = values[f]
            if i == 0:
                parts = [list(values), list(values), list(cell), list(cell)]
            else:
                for f in range(fields):
                    parts[0][f] = r * parts[0][f] + values[f]
                    parts[1][f] = parts[1][f] + (r**i) * values[f]
                    parts[2][f] = q * parts[2][f] + cell[f]
                    parts[3][f] = parts[3][f] + (q**i) * cell[f]
        for s in range(4):
            for f in range(fields):
                sums[s, f, at, :] = parts[s][f]
        return carry

    lax.fori_loop(0, tiles, flux_tile, 0, unroll=True)

    sum_copies = [
        remote(sums, got_sums.at[step - 1], 3 + step, pitch=lax.rem(pitch + step, npitch))
        for step in range(1, npitch)
    ]
    for copy in sum_copies:
        copy.start()

    when(jnp.logical_not(has_up), lambda: clear(got_tail))
    when(jnp.logical_not(has_down), lambda: clear(got_head))
    when(jnp.logical_not(has_left), lambda: clear(got_left))
    when(jnp.logical_not(has_right), lambda: clear(got_right))

    weight = -DAMPING / 256.0

    def damp_field(f, carry):
        for i in range(cells):
            x = u[f, i]
            result = (140.0 * weight) * x
            for o, c in ((1, -56.0), (2, 28.0), (3, -8.0), (4, 1.0)):
                pair = (pltpu.roll(x, o, 0) + pltpu.roll(x, rows - o, 0)) + (
                    pltpu.roll(x, o, 1) + pltpu.roll(x, 128 - o, 1)
                )
                result = result + (c * weight) * pair
            out_ref[f, i] = result
        return carry

    lax.fori_loop(0, fields, damp_field, 0, unroll=True)

    for copy in small_copies:
        copy.wait()
    order = row.astype(jnp.float32) + 1.0
    phase = (2.0 * math.pi / PERIOD_SAMPLES) * order * lag_ref[0].astype(jnp.float32)
    active = row < harm_ref[...]
    waves[0] = jnp.where(active, jnp.cos(phase), 0.0)
    waves[1] = jnp.where(active, jnp.sin(phase), 0.0)
    near_first = pick(pitch, [r ** (cells * p) for p in range(npitch)])
    near_last = pick(pitch, [r ** (cells * (npitch - 1 - p)) for p in range(npitch)])
    jump_scale = -STEP_RATE * 0.75 * r_scale / (1.0 - r**total)
    jump_weights = [
        near_first * (jump_scale * (r**i + r ** (i + 1)))
        + near_last * (jump_scale * (r ** (cells - i) + r ** (cells - 1 - i)))
        for i in range(cells)
    ]
    flux_scale = -STEP_RATE * 0.75 * r_scale * (r - 1.0 / r)

    coef_copy.wait()

    def solve_field(f, carry):
        for t in range(tiles):
            at = pl.ds(t * 8, 8)
            jump = None
            for part in range(2):
                for k in range(harm_max):
                    term = waves[part, pl.ds(k, 1), :] * co[part, k, f, at, :]
                    jump = term if jump is None else jump + term
            x = [u[f, i, at, :] for i in range(cells)]
            y = [flux[f, i, at, :] for i in range(cells)]
            back_x, back_y = [None] * cells, [None] * cells
            carry_x, carry_y = q * x[cells - 1], y[cells - 1]
            for i in reversed(range(cells - 1)):
                back_x[i], back_y[i] = carry_x, carry_y
                if i > 0:
                    carry_x = q * (x[i] + carry_x)
                    carry_y = y[i] + r * carry_y
            front_x, front_y = None, None
            for i in range(cells):
                front_x = x[i] if front_x is None else x[i] + q * front_x
                value = out_ref[f, i, at, :] + jump_weights[i] * jump
                relaxed = front_x if back_x[i] is None else front_x + back_x[i]
                value = value + q_scale * relaxed
                slope = front_y
                if back_y[i] is not None:
                    slope = -back_y[i] if slope is None else slope - back_y[i]
                value = value + (flux_scale * r) * slope
                front_y = y[i] if front_y is None else y[i] + r * front_y
                out_ref[f, i, at, :] = value
        return carry

    lax.fori_loop(0, fields, solve_field, 0, unroll=True)

    for copy in sum_copies:
        copy.wait_recv()
    r_wrap = 1.0 / (1.0 - r**total)
    q_wrap = 1.0 / (1.0 - q**total)

    def carry_field(f, carry):
        for t in range(tiles):
            at = pl.ds(t * 8, 8)
            joined = []
            for s, (root, wrap) in enumerate(
                ((r, r_wrap), (r, r_wrap), (q, q_wrap), (q, q_wrap))
            ):
                value = (wrap * root ** (cells * (npitch - 1))) * sums[s, f, at, :]
                for step in range(1, npitch):
                    distance = step - 1 if s % 2 == 0 else npitch - 1 - step
                    factor = wrap * root ** (cells * distance)
                    value = value + factor * got_sums[step - 1, s, f, at, :]
                joined.append(value)
            for i in range(cells):
                out_ref[f, i, at, :] = (
                    out_ref[f, i, at, :]
                    + (flux_scale * r ** (i + 1)) * joined[0]
                    - (flux_scale * r ** (cells - i)) * joined[1]
                    + (q_scale * q ** (i + 1)) * joined[2]
                    + (q_scale * q ** (cells - i)) * joined[3]
                )
        return carry

    lax.fori_loop(0, fields, carry_field, 0, unroll=True)

    when(has_left, right_copy.wait_recv)
    when(has_right, left_copy.wait_recv)
    place = lane % 8
    outer = jnp.logical_or(lane < 4, lane >= 124)

    def span_field(f, carry):
        for g in range(sp_own.shape[1]):
            delta = jnp.where(place < 4, got_left[f, g], got_right[f, g]) - sp_own[f, g]
            ends = jnp.zeros((8, 128), jnp.float32)
            for t in range(4):
                ends = ends + jnp.where(
                    jnp.logical_and(place >= 4, place + t < 8),
                    EDGE[t] * weight,
                    0.0,
                ) * pltpu.roll(delta, 4 - t, 1)
                ends = ends + jnp.where(
                    jnp.logical_and(place < 4, place >= t),
                    EDGE[t] * weight,
                    0.0,
                ) * pltpu.roll(delta, 124 + t, 1)
            for k in range(16):
                i, t = g * half + k // tiles, k % tiles
                moved = pltpu.roll(ends, (124 - 8 * k) % 128, 1)
                out_ref[f, i, t * 8 : t * 8 + 8, :] += jnp.where(outer, moved, 0.0)
        return carry

    lax.fori_loop(0, fields, span_field, 0, unroll=True)

    when(has_up, down_copy.wait_recv)
    when(has_down, up_copy.wait_recv)
    step_row = row % 4

    def axial_field(f, carry):
        for k in range(cells // 2):
            delta = got_tail[f, k] - ax_tail[f, k]
            ends = (EDGE[0] * weight) * delta
            for t in range(1, 4):
                ends = ends + jnp.where(step_row + t < 4, EDGE[t] * weight, 0.0) * pltpu.roll(
                    delta, 8 - t, 0
                )
            out_ref[f, 2 * k, :8, :] += jnp.where(low_rows, ends, 0.0)
            out_ref[f, 2 * k + 1, :8, :] += jnp.where(low_rows, pltpu.roll(ends, 4, 0), 0.0)
            delta = got_head[f, k] - ax_head[f, k]
            ends = (EDGE[0] * weight) * delta
            for t in range(1, 4):
                ends = ends + jnp.where(step_row >= t, EDGE[t] * weight, 0.0) * pltpu.roll(
                    delta, t, 0
                )
            out_ref[f, 2 * k, rows - 8 :, :] += jnp.where(low_rows, 0.0, pltpu.roll(ends, 4, 0))
            out_ref[f, 2 * k + 1, rows - 8 :, :] += jnp.where(low_rows, 0.0, ends)
        return carry

    lax.fori_loop(0, fields, axial_field, 0, unroll=True)

    for copy in sum_copies:
        copy.wait_send()
    when(has_down, down_copy.wait_send)
    when(has_up, up_copy.wait_send)
    when(has_right, right_copy.wait_send)
    when(has_left, left_copy.wait_send)


def shards(sizes, state, coeffs, lag_shift, harmonics):
    fields, cells, rows, lanes = state.shape
    npitch = sizes[0]
    groups = cells * (rows // 8) // 16
    vmem = lambda *shape: pltpu.VMEM(shape, jnp.float32)
    halo = (fields, cells // 2, 8, lanes)
    packed = (fields, groups, 8, lanes)
    sems = 4 + npitch - 1
    return pl.pallas_call(
        functools.partial(kernel, sizes),
        out_shape=pltpu.VMEM(state.shape, jnp.float32),
        in_specs=[
            pl.BlockSpec(memory_space=pltpu.HBM),
            pl.BlockSpec(memory_space=pltpu.HBM),
            pl.BlockSpec(memory_space=pltpu.HBM),
            pl.BlockSpec(memory_space=pltpu.HBM),
        ],
        out_specs=pl.BlockSpec(memory_space=pltpu.VMEM),
        scratch_shapes=[
            vmem(*state.shape),
            vmem(*coeffs.shape),
            vmem(*state.shape),
            vmem(4, fields, rows, lanes),
            vmem(npitch - 1, 4, fields, rows, lanes),
            vmem(*halo),
            vmem(*halo),
            vmem(*halo),
            vmem(*halo),
            vmem(*packed),
            vmem(*packed),
            vmem(*packed),
            vmem(2, 8, lanes),
            pltpu.SMEM((1,), jnp.int32),
            pltpu.VMEM((1, lanes), jnp.int32),
            pltpu.SemaphoreType.DMA((4,)),
            pltpu.SemaphoreType.DMA((sems,)),
            pltpu.SemaphoreType.DMA((sems,)),
        ],
        compiler_params=pltpu.CompilerParams(collective_id=0, has_side_effects=True),
    )(lag_shift, harmonics.reshape(1, lanes), state, coeffs)


def solution(mesh):
    sizes = tuple(mesh.shape[name] for name in ("pitch", "axial", "span"))
    placed = (
        P(None, "pitch", "axial", "span"),
        P(None, None, None, "axial", "span"),
        P(),
        P("span"),
    )
    return jax.shard_map(
        functools.partial(shards, sizes),
        mesh=mesh,
        in_specs=placed,
        out_specs=P(None, "pitch", "axial", "span"),
        check_vma=False,
    )
```

profile of v0, /device:TPU:0, one launch (start us, length us, event | category | flops | bytes accessed | tf_op | source)
XLA Modules:
  0.0 9.4 jit_solution(1427400801693109844)
XLA Ops:
  0.7 7.9 %shard_map.46 = f32[5,8,32,128]{3,2,1,0:T(8,128)S(1)} custom-call(s32[1]{0:T(128)S(6)} %copy.7.lag_hbm, s32[1,128]{1,0:T(1,128)} %bitcast.1, f32[5,8,32,128]{3,2,1,0:T(8,128)} %state_hbm.1, f32[2,4,5,32,128]{4,3,2,1,0:T(8,128)} %coef_hbm.1), custom_call_target="tpu_custom_call" | custom-call | tf_op jit(solution)/shard_map/pallas_call | solution.py:383
  8.5 0.8 %copy.6 = f32[5,8,32,128]{3,2,1,0:T(8,128)} copy(f32[5,8,32,128]{3,2,1,0:T(8,128)S(1)} %shard_map.46) | data formatting | bytes 1310720
where the time goes:
time: 9.52 us; the launch traced here: 9.36 us
  Pallas kernels  7.86 us (83%)
  local copies, waits for them, and re-layouts  0.84 us (9%)
  between operations  0.66 us (7%)
    pallas_call x1, Pallas kernels, shards(): pl.pallas_call(functools.partial(kernel, sizes), out_shape=pltpu.VMEM(sta...  7.86 us
    unnamed x1, local copies, waits for them, and re-layouts  0.84 us

commit v1 on v0

--- a/solution.py
+++ b/solution.py
@@ -40,16 +40,18 @@
     flux,
     sums,
     got_sums,
-    ax_tail,
-    ax_head,
-    got_tail,
-    got_head,
+    ax_own,
+    ax_got,
     sp_own,
     got_left,
     got_right,
     waves,
     lag_ref,
     harm_ref,
+    pitch_ready,
+    span_ready,
+    odd_ready,
+    even_ready,
     local_sem,
     send_sem,
     recv_sem,
@@ -64,65 +66,71 @@
     q, q_scale = line_root(1.0 + 2.0 * diffusion, -diffusion)
     pitch, axial, span = (lax.axis_index(name) for name in ("pitch", "axial", "span"))
 
-    state_copy = pltpu.make_async_copy(state_hbm, u, local_sem.at[0])
-    coef_copy = pltpu.make_async_copy(coef_hbm, co, local_sem.at[1])
-    state_copy.start()
-
-    barrier = pltpu.get_barrier_semaphore()
-
-    def greet(**where):
-        pl.semaphore_signal(barrier, inc=1, device_id=where, device_id_type=MESH)
-
+    state_copies = [
+        pltpu.make_async_copy(state_hbm.at[f], u.at[f], local_sem.at[3 + f]) for f in range(fields)
+    ]
+    coef_copy = pltpu.make_async_copy(coef_hbm, co, local_sem.at[0])
+    small_copies = [
+        pltpu.make_async_copy(lag_hbm, lag_ref, local_sem.at[1]),
+        pltpu.make_async_copy(harm_hbm, harm_ref, local_sem.at[2]),
+    ]
+
+    def when(flag, action):
+        @pl.when(flag)
+        def _():
+            action()
+
+    def both(*flags):
+        return functools.reduce(jnp.logical_and, flags)
+
+    def no(flag):
+        return jnp.logical_not(flag)
+
+    paired = npitch % 2 == 0
     has_up, has_down = axial > 0, axial < naxial - 1
     has_left, has_right = span > 0, span < nspan - 1
-
-    @pl.when(has_up)
-    def _():
-        greet(axial=axial - 1)
-
-    @pl.when(has_down)
-    def _():
-        greet(axial=axial + 1)
-
-    @pl.when(has_left)
-    def _():
-        greet(span=span - 1)
-
-    @pl.when(has_right)
-    def _():
-        greet(span=span + 1)
-
-    for step in range(1, npitch):
-        greet(pitch=lax.rem(pitch + step, npitch))
-    coef_copy.start()
-    small_copies = [
-        pltpu.make_async_copy(lag_hbm, lag_ref, local_sem.at[2]),
-        pltpu.make_async_copy(harm_hbm, harm_ref, local_sem.at[3]),
-    ]
-    for copy in small_copies:
+    odd = lax.rem(axial, 2) == 1
+    even = no(odd)
+    hub_block = both(even, axial + 2 < naxial)
+    last_even = both(even, axial + 2 >= naxial)
+    second = lax.rem(pitch, 2) == 1 if paired else pitch >= 0
+    first = no(second)
+    hub = both(hub_block, second)
+    under_hub = both(odd, has_down)
+
+    barrier = pltpu.get_barrier_semaphore()
+
+    def tell(semaphore, **where):
+        pl.semaphore_signal(semaphore, inc=1, device_id=where, device_id_type=MESH)
+
+    def count(*flags):
+        return sum(jnp.where(flag, 1, 0) for flag in flags)
+
+    when(both(odd, no(both(has_down, first))), lambda: tell(barrier, axial=axial - 1))
+    when(under_hub, lambda: tell(barrier, axial=axial + 1))
+    when(both(even, has_down), lambda: tell(barrier, axial=axial + 1))
+    when(both(even, has_up, second), lambda: tell(barrier, axial=axial - 2))
+    if paired:
+        when(both(under_hub, first), lambda: tell(barrier, axial=axial - 1, pitch=pitch + 1))
+        when(both(even, has_up, first), lambda: tell(barrier, axial=axial - 2, pitch=pitch + 1))
+    when(has_right, lambda: tell(barrier, span=span + 1))
+    when(both(last_even, has_left), lambda: tell(barrier, span=span - 1))
+    for other in range(npitch - 1):
+        when(other < pitch, lambda: tell(barrier, pitch=jnp.int32(other)))
+    for copy in state_copies:
         copy.start()
 
-    row = lax.broadcasted_iota(jnp.int32, (8, 128), 0)
-    lane = lax.broadcasted_iota(jnp.int32, (8, 128), 1)
-    group = lane // 8
-    low_rows = row < 4
-
-    state_copy.wait()
-
-    def pack_axial(f, carry):
-        for k in range(cells // 2):
-            a, b = u[f, 2 * k, rows - 8 :, :], u[f, 2 * k + 1, rows - 8 :, :]
-            ax_tail[f, k] = jnp.where(low_rows, pltpu.roll(a, 4, 0), b)
-            a, b = u[f, 2 * k, :8, :], u[f, 2 * k + 1, :8, :]
-            ax_head[f, k] = jnp.where(low_rows, a, pltpu.roll(b, 4, 0))
-        return carry
-
-    lax.fori_loop(0, fields, pack_axial, 0, unroll=True)
-
-    neighbours = npitch - 1
-    for flag in (has_up, has_down, has_left, has_right):
-        neighbours = neighbours + jnp.where(flag, 1, 0)
-    pl.semaphore_wait(barrier, neighbours)
+    heard = count(has_left, both(last_even, has_right), has_up, both(last_even, has_down))
+    heard = heard + count(hub, hub) * (2 if paired else 1) + (npitch - 1 - pitch)
+    pl.semaphore_wait(barrier, heard)
+
+    when(both(under_hub, first), lambda: tell(even_ready, axial=axial - 1))
+    when(hub, lambda: tell(odd_ready, axial=axial + 1))
+    if paired:
+        when(hub, lambda: tell(odd_ready, axial=axial + 1, pitch=pitch - 1))
+    when(both(has_left, no(last_even)), lambda: tell(span_ready, span=span - 1))
+    for other in range(1, npitch):
+        when(other > pitch, lambda: tell(pitch_ready, pitch=jnp.int32(other)))
 
     def remote(src, dst, slot, **where):
         return pltpu.make_async_remote_copy(
@@ -134,23 +142,23 @@
             device_id_type=MESH,
         )
 
-    down_copy = remote(ax_tail, got_tail, 0, axial=axial + 1)
-    up_copy = remote(ax_head, got_head, 1, axial=axial - 1)
+    down_copy = remote(
+        state_hbm.at[:, :, rows - 4 :, :], ax_got.at[:, :, :4, :], 0, axial=axial + 1
+    )
+    up_copy = remote(state_hbm.at[:, :, :4, :], ax_got.at[:, :, 4:, :], 1, axial=axial - 1)
     right_copy = remote(sp_own, got_left, 2, span=span + 1)
     left_copy = remote(sp_own, got_right, 3, span=span - 1)
 
-    def when(flag, action):
-        @pl.when(flag)
-        def _():
-            action()
-
-    def clear(ref):
-        ref[...] = jnp.zeros_like(ref)
-
-    odd = lax.rem(axial, 2) == 1
-    when(jnp.logical_and(has_up, odd), up_copy.start)
-    when(has_down, down_copy.start)
-    when(jnp.logical_and(has_up, jnp.logical_not(odd)), up_copy.start)
+    when(has_up, up_copy.start)
+    when(both(has_down, no(odd), no(both(hub_block, first))), down_copy.start)
+    coef_copy.start()
+    for copy in small_copies:
+        copy.start()
+
+    row = lax.broadcasted_iota(jnp.int32, (8, 128), 0)
+    lane = lax.broadcasted_iota(jnp.int32, (8, 128), 1)
+    group = lane // 8
+    low_rows = row < 4
 
     half = cells // (sp_own.shape[1])
 
@@ -163,9 +171,11 @@
             sp_own[f, g] = packed
         return carry
 
-    lax.fori_loop(0, fields, pack_span, 0, unroll=True)
-    when(has_right, right_copy.start)
+    for f in range(fields):
+        state_copies[f].wait()
+        pack_span(f, 0)
     when(has_left, left_copy.start)
+    when(both(has_right, last_even), right_copy.start)
 
     def flux_tile(t, carry):
         at = pl.ds(pl.multiple_of(t * 8, 8), 8)
@@ -204,13 +214,17 @@
         remote(sums, got_sums.at[step - 1], 3 + step, pitch=lax.rem(pitch + step, npitch))
         for step in range(1, npitch)
     ]
+    when(pitch > 0, lambda: pl.semaphore_wait(pitch_ready, pitch))
     for copy in sum_copies:
         copy.start()
 
-    when(jnp.logical_not(has_up), lambda: clear(got_tail))
-    when(jnp.logical_not(has_down), lambda: clear(got_head))
-    when(jnp.logical_not(has_left), lambda: clear(got_left))
-    when(jnp.logical_not(has_right), lambda: clear(got_right))
+    def clear(ref):
+        ref[...] = jnp.zeros_like(ref)
+
+    when(no(has_up), lambda: clear(ax_got.at[:, :, :4, :]))
+    when(no(has_down), lambda: clear(ax_got.at[:, :, 4:, :]))
+    when(no(has_left), lambda: clear(got_left))
+    when(no(has_right), lambda: clear(got_right))
 
     weight = -DAMPING / 256.0
 
@@ -224,9 +238,31 @@
                 )
                 result = result + (c * weight) * pair
             out_ref[f, i] = result
-        return carry
-
-    lax.fori_loop(0, fields, damp_field, 0, unroll=True)
+            ends = jnp.where(low_rows, x[:8, :], x[rows - 8 :, :])
+            ax_own[f, i] = -pltpu.roll(ends, 4, 0)
+        return carry
+
+    damp_field(0, 0)
+
+    @pl.when(under_hub)
+    def _():
+        pl.semaphore_wait(odd_ready, 1)
+        down_copy.start()
+
+    @pl.when(both(hub_block, first))
+    def _():
+        pl.semaphore_wait(even_ready, 1)
+        down_copy.start()
+
+    damp_field(1, 0)
+
+    @pl.when(both(has_right, no(last_even)))
+    def _():
+        pl.semaphore_wait(span_ready, 1)
+        right_copy.start()
+
+    for f in range(2, fields):
+        damp_field(f, 0)
 
     for copy in small_copies:
         copy.wait()
@@ -340,26 +376,18 @@
 
     when(has_up, down_copy.wait_recv)
     when(has_down, up_copy.wait_recv)
-    step_row = row % 4
+    near_low = [jnp.where(row + t < 4, EDGE[t] * weight, 0.0) for t in range(1, 4)]
+    near_high = [jnp.where(row >= 4 + t, EDGE[t] * weight, 0.0) for t in range(1, 4)]
 
     def axial_field(f, carry):
-        for k in range(cells // 2):
-            delta = got_tail[f, k] - ax_tail[f, k]
+        for i in range(cells):
+            delta = ax_got[f, i] + ax_own[f, i]
             ends = (EDGE[0] * weight) * delta
             for t in range(1, 4):
-                ends = ends + jnp.where(step_row + t < 4, EDGE[t] * weight, 0.0) * pltpu.roll(
-                    delta, 8 - t, 0
-                )
-            out_ref[f, 2 * k, :8, :] += jnp.where(low_rows, ends, 0.0)
-            out_ref[f, 2 * k + 1, :8, :] += jnp.where(low_rows, pltpu.roll(ends, 4, 0), 0.0)
-            delta = got_head[f, k] - ax_head[f, k]
-            ends = (EDGE[0] * weight) * delta
-            for t in range(1, 4):
-                ends = ends + jnp.where(step_row >= t, EDGE[t] * weight, 0.0) * pltpu.roll(
-                    delta, t, 0
-                )
-            out_ref[f, 2 * k, rows - 8 :, :] += jnp.where(low_rows, 0.0, pltpu.roll(ends, 4, 0))
-            out_ref[f, 2 * k + 1, rows - 8 :, :] += jnp.where(low_rows, 0.0, ends)
+                ends = ends + near_low[t - 1] * pltpu.roll(delta, 8 - t, 0)
+                ends = ends + near_high[t - 1] * pltpu.roll(delta, t, 0)
+            out_ref[f, i, :8, :] += jnp.where(low_rows, ends, 0.0)
+            out_ref[f, i, rows - 8 :, :] += jnp.where(low_rows, 0.0, ends)
         return carry
 
     lax.fori_loop(0, fields, axial_field, 0, unroll=True)
@@ -377,7 +405,7 @@
     npitch = sizes[0]
     groups = cells * (rows // 8) // 16
     vmem = lambda *shape: pltpu.VMEM(shape, jnp.float32)
-    halo = (fields, cells // 2, 8, lanes)
+    halo = (fields, cells, 8, lanes)
     packed = (fields, groups, 8, lanes)
     sems = 4 + npitch - 1
     return pl.pallas_call(
@@ -398,15 +426,17 @@
             vmem(npitch - 1, 4, fields, rows, lanes),
             vmem(*halo),
             vmem(*halo),
-            vmem(*halo),
-            vmem(*halo),
             vmem(*packed),
             vmem(*packed),
             vmem(*packed),
             vmem(2, 8, lanes),
             pltpu.SMEM((1,), jnp.int32),
             pltpu.VMEM((1, lanes), jnp.int32),
-            pltpu.SemaphoreType.DMA((4,)),
+            pltpu.SemaphoreType.REGULAR,
+            pltpu.SemaphoreType.REGULAR,
+            pltpu.SemaphoreType.REGULAR,
+            pltpu.SemaphoreType.REGULAR,
+            pltpu.SemaphoreType.DMA((3 + fields,)),
             pltpu.SemaphoreType.DMA((sems,)),
             pltpu.SemaphoreType.DMA((sems,)),
         ],

time: 9.52 us -> 9.64 us (1.013)
  Pallas kernels: 7.86 us -> 7.98 us
    pallas_call x1, Pallas kernels: 7.86 us -> 7.98 us  [shards(): pl.pallas_call(functools.partial(kernel, sizes), out_shape=pltpu.VMEM(sta...]
where the time goes in v1:
time: 9.64 us; the launch traced here: 9.48 us
  Pallas kernels  7.98 us (83%)
  local copies, waits for them, and re-layouts  0.84 us (9%)
  between operations  0.66 us (7%)
    pallas_call x1, Pallas kernels, shards(): pl.pallas_call(functools.partial(kernel, sizes), out_shape=pltpu.VMEM(sta...  7.98 us
    unnamed x1, local copies, waits for them, and re-layouts  0.84 us

profile of v1, /device:TPU:0, one launch (start us, length us, event | category | flops | bytes accessed | tf_op | source)
XLA Modules:
  0.0 9.5 jit_solution(17610121360193738590)
XLA Ops:
  0.7 8.0 %shard_map.46 = f32[5,8,32,128]{3,2,1,0:T(8,128)S(1)} custom-call(s32[1]{0:T(128)S(6)} %copy.7.lag_hbm, s32[1,128]{1,0:T(1,128)} %bitcast.1, f32[5,8,32,128]{3,2,1,0:T(8,128)} %state_hbm.1, f32[2,4,5,32,128]{4,3,2,1,0:T(8,128)} %coef_hbm.1), custom_call_target="tpu_custom_call" | custom-call | tf_op jit(solution)/shard_map/pallas_call | solution.py:411
  8.6 0.8 %copy.6 = f32[5,8,32,128]{3,2,1,0:T(8,128)} copy(f32[5,8,32,128]{3,2,1,0:T(8,128)S(1)} %shard_map.46) | data formatting | bytes 1310720

commit v2 on v1

--- a/solution.py
+++ b/solution.py
@@ -42,7 +42,8 @@
     got_sums,
     ax_own,
     ax_got,
-    sp_own,
+    sp_left,
+    sp_right,
     got_left,
     got_right,
     waves,
@@ -142,37 +143,42 @@
             device_id_type=MESH,
         )
 
-    down_copy = remote(
-        state_hbm.at[:, :, rows - 4 :, :], ax_got.at[:, :, :4, :], 0, axial=axial + 1
-    )
-    up_copy = remote(state_hbm.at[:, :, :4, :], ax_got.at[:, :, 4:, :], 1, axial=axial - 1)
-    right_copy = remote(sp_own, got_left, 2, span=span + 1)
-    left_copy = remote(sp_own, got_right, 3, span=span - 1)
-
-    when(has_up, up_copy.start)
-    when(both(has_down, no(odd), no(both(hub_block, first))), down_copy.start)
+    down_copy = remote(u.at[:, :, rows - 4 :, :], ax_got.at[:, :, :4, :], 0, axial=axial + 1)
+    up_copy = remote(u.at[:, :, :4, :], ax_got.at[:, :, 4:, :], 1, axial=axial - 1)
+    soon_copy = remote(state_hbm.at[:, :, :4, :], ax_got.at[:, :, 4:, :], 1, axial=axial - 1)
+    right_copy = remote(sp_right, got_left, 2, span=span + 1)
+    left_copy = remote(sp_left, got_right, 3, span=span - 1)
+
+    when(odd, soon_copy.start)
     coef_copy.start()
     for copy in small_copies:
         copy.start()
 
     row = lax.broadcasted_iota(jnp.int32, (8, 128), 0)
     lane = lax.broadcasted_iota(jnp.int32, (8, 128), 1)
-    group = lane // 8
+    group, place = lane // 4, lane % 4
     low_rows = row < 4
 
-    half = cells // (sp_own.shape[1])
+    for copy in state_copies:
+        copy.wait()
+    when(both(has_up, even), up_copy.start)
+    when(both(has_down, even, no(both(hub_block, first))), down_copy.start)
+
+    groups = sp_left.shape[1]
 
     def pack_span(f, carry):
-        for g in range(sp_own.shape[1]):
-            packed = jnp.zeros((8, 128), jnp.float32)
-            for k in range(16):
-                tile = u[f, g * half + k // tiles, (k % tiles) * 8 : (k % tiles) * 8 + 8, :]
-                packed = jnp.where(group == k, pltpu.roll(tile, (8 * k + 4) % 128, 1), packed)
-            sp_own[f, g] = packed
+        for g in range(groups):
+            right = left = jnp.zeros((8, 128), jnp.float32)
+            for k in range(32):
+                i, t = divmod(g * 32 + k, tiles)
+                moved = pltpu.roll(u[f, i, t * 8 : t * 8 + 8, :], (4 * k + 4) % 128, 1)
+                right = jnp.where(group == k, moved, right)
+                left = jnp.where(group == (k + 1) % 32, moved, left)
+            sp_right[f, g] = right
+            sp_left[f, g] = left
         return carry
 
     for f in range(fields):
-        state_copies[f].wait()
         pack_span(f, 0)
     when(has_left, left_copy.start)
     when(both(has_right, last_even), right_copy.start)
@@ -348,27 +354,27 @@
 
     when(has_left, right_copy.wait_recv)
     when(has_right, left_copy.wait_recv)
-    place = lane % 8
     outer = jnp.logical_or(lane < 4, lane >= 124)
+    from_left = [jnp.where(place + t < 4, EDGE[t] * weight, 0.0) for t in range(4)]
+    from_right = [jnp.where(place >= t, EDGE[t] * weight, 0.0) for t in range(4)]
+    even_group = group % 2 == 0
 
     def span_field(f, carry):
-        for g in range(sp_own.shape[1]):
-            delta = jnp.where(place < 4, got_left[f, g], got_right[f, g]) - sp_own[f, g]
-            ends = jnp.zeros((8, 128), jnp.float32)
-            for t in range(4):
-                ends = ends + jnp.where(
-                    jnp.logical_and(place >= 4, place + t < 8),
-                    EDGE[t] * weight,
-                    0.0,
-                ) * pltpu.roll(delta, 4 - t, 1)
-                ends = ends + jnp.where(
-                    jnp.logical_and(place < 4, place >= t),
-                    EDGE[t] * weight,
-                    0.0,
-                ) * pltpu.roll(delta, 124 + t, 1)
-            for k in range(16):
-                i, t = g * half + k // tiles, k % tiles
-                moved = pltpu.roll(ends, (124 - 8 * k) % 128, 1)
+        for g in range(groups):
+            before = got_left[f, g] - sp_right[f, g]
+            after = got_right[f, g] - sp_left[f, g]
+            starts, stops = from_left[0] * before, from_right[0] * after
+            for t in range(1, 4):
+                starts = starts + from_left[t] * pltpu.roll(before, 128 - t, 1)
+                stops = stops + from_right[t] * pltpu.roll(after, t, 1)
+            stops = pltpu.roll(stops, 120, 1)
+            ends = (
+                jnp.where(even_group, starts, stops),
+                jnp.where(even_group, stops, starts),
+            )
+            for k in range(32):
+                i, t = divmod(g * 32 + k, tiles)
+                moved = pltpu.roll(ends[k % 2], (128 - 4 * k) % 128, 1)
                 out_ref[f, i, t * 8 : t * 8 + 8, :] += jnp.where(outer, moved, 0.0)
         return carry
 
@@ -403,7 +409,7 @@
 def shards(sizes, state, coeffs, lag_shift, harmonics):
     fields, cells, rows, lanes = state.shape
     npitch = sizes[0]
-    groups = cells * (rows // 8) // 16
+    groups = cells * (rows // 8) // 32
     vmem = lambda *shape: pltpu.VMEM(shape, jnp.float32)
     halo = (fields, cells, 8, lanes)
     packed = (fields, groups, 8, lanes)
@@ -429,6 +435,7 @@
             vmem(*packed),
             vmem(*packed),
             vmem(*packed),
+            vmem(*packed),
             vmem(2, 8, lanes),
             pltpu.SMEM((1,), jnp.int32),
             pltpu.VMEM((1, lanes), jnp.int32),

time: 9.64 us -> 8.68 us (0.900)
  Pallas kernels: 7.98 us -> 7.02 us
    pallas_call x1, Pallas kernels: 7.98 us -> 7.02 us  [shards(): pl.pallas_call(functools.partial(kernel, sizes), out_shape=pltpu.VMEM(sta...]
where the time goes in v2:
time: 8.68 us; the launch traced here: 8.52 us
  Pallas kernels  7.02 us (81%)
  local copies, waits for them, and re-layouts  0.84 us (10%)
  between operations  0.66 us (8%)
    pallas_call x1, Pallas kernels, shards(): pl.pallas_call(functools.partial(kernel, sizes), out_shape=pltpu.VMEM(sta...  7.02 us
    unnamed x1, local copies, waits for them, and re-layouts  0.84 us

profile of v2, /device:TPU:0, one launch (start us, length us, event | category | flops | bytes accessed | tf_op | source)
XLA Modules:
  0.0 8.5 jit_solution(6367396822917705950)
XLA Ops:
  0.7 7.0 %shard_map.46 = f32[5,8,32,128]{3,2,1,0:T(8,128)S(1)} custom-call(s32[1]{0:T(128)S(6)} %copy.7.lag_hbm, s32[1,128]{1,0:T(1,128)} %bitcast.1, f32[5,8,32,128]{3,2,1,0:T(8,128)} %state_hbm.1, f32[2,4,5,32,128]{4,3,2,1,0:T(8,128)} %coef_hbm.1), custom_call_target="tpu_custom_call" | custom-call | tf_op jit(solution)/shard_map/pallas_call | solution.py:417
  7.7 0.8 %copy.6 = f32[5,8,32,128]{3,2,1,0:T(8,128)} copy(f32[5,8,32,128]{3,2,1,0:T(8,128)S(1)} %shard_map.46) | data formatting | bytes 1310720

commit v3 on v2

--- a/solution.py
+++ b/solution.py
@@ -19,6 +19,11 @@
 def line_root(main, side):
     root = (-main + math.sqrt(main * main - 4.0 * side * side)) / (2.0 * side)
     return root, 1.0 / (main + 2.0 * side * root)
+
+
+def split(fields):
+    cuts = sorted({0, fields * 2 // 5, fields * 4 // 5, fields})
+    return tuple(zip(cuts[:-1], cuts[1:]))
 
 
 def pick(position, values):
@@ -51,8 +56,7 @@
     harm_ref,
     pitch_ready,
     span_ready,
-    odd_ready,
-    even_ready,
+    next_ready,
     local_sem,
     send_sem,
     recv_sem,
@@ -60,6 +64,7 @@
     npitch, naxial, nspan = sizes
     fields, cells, rows, _ = u.shape
     tiles = rows // 8
+    parts = split(fields)
     harm_max = co.shape[1]
     total = cells * npitch
     diffusion = float(total * total // 64)
@@ -67,9 +72,7 @@
     q, q_scale = line_root(1.0 + 2.0 * diffusion, -diffusion)
     pitch, axial, span = (lax.axis_index(name) for name in ("pitch", "axial", "span"))
 
-    state_copies = [
-        pltpu.make_async_copy(state_hbm.at[f], u.at[f], local_sem.at[3 + f]) for f in range(fields)
-    ]
+    state_copy = pltpu.make_async_copy(state_hbm, u, local_sem.at[3])
     coef_copy = pltpu.make_async_copy(coef_hbm, co, local_sem.at[0])
     small_copies = [
         pltpu.make_async_copy(lag_hbm, lag_ref, local_sem.at[1]),
@@ -99,6 +102,7 @@
     hub = both(hub_block, second)
     under_hub = both(odd, has_down)
 
+    state_copy.start()
     barrier = pltpu.get_barrier_semaphore()
 
     def tell(semaphore, **where):
@@ -107,31 +111,21 @@
     def count(*flags):
         return sum(jnp.where(flag, 1, 0) for flag in flags)
 
-    when(both(odd, no(both(has_down, first))), lambda: tell(barrier, axial=axial - 1))
-    when(under_hub, lambda: tell(barrier, axial=axial + 1))
-    when(both(even, has_down), lambda: tell(barrier, axial=axial + 1))
-    when(both(even, has_up, second), lambda: tell(barrier, axial=axial - 2))
+    heard_by = pitch
     if paired:
-        when(both(under_hub, first), lambda: tell(barrier, axial=axial - 1, pitch=pitch + 1))
-        when(both(even, has_up, first), lambda: tell(barrier, axial=axial - 2, pitch=pitch + 1))
+        heard_by = jnp.where(both(first, jnp.logical_or(even, has_down)), pitch + 1, pitch)
+    when(
+        has_up,
+        lambda: tell(barrier, axial=jnp.where(odd, axial - 1, axial - 2), pitch=heard_by),
+    )
+    when(has_down, lambda: tell(barrier, axial=axial + 1))
     when(has_right, lambda: tell(barrier, span=span + 1))
-    when(both(last_even, has_left), lambda: tell(barrier, span=span - 1))
     for other in range(npitch - 1):
         when(other < pitch, lambda: tell(barrier, pitch=jnp.int32(other)))
-    for copy in state_copies:
-        copy.start()
-
-    heard = count(has_left, both(last_even, has_right), has_up, both(last_even, has_down))
+
+    heard = count(has_left, has_up, both(last_even, has_down))
     heard = heard + count(hub, hub) * (2 if paired else 1) + (npitch - 1 - pitch)
     pl.semaphore_wait(barrier, heard)
-
-    when(both(under_hub, first), lambda: tell(even_ready, axial=axial - 1))
-    when(hub, lambda: tell(odd_ready, axial=axial + 1))
-    if paired:
-        when(hub, lambda: tell(odd_ready, axial=axial + 1, pitch=pitch - 1))
-    when(both(has_left, no(last_even)), lambda: tell(span_ready, span=span - 1))
-    for other in range(1, npitch):
-        when(other > pitch, lambda: tell(pitch_ready, pitch=jnp.int32(other)))
 
     def remote(src, dst, slot, **where):
         return pltpu.make_async_remote_copy(
@@ -143,26 +137,45 @@
             device_id_type=MESH,
         )
 
-    down_copy = remote(u.at[:, :, rows - 4 :, :], ax_got.at[:, :, :4, :], 0, axial=axial + 1)
-    up_copy = remote(u.at[:, :, :4, :], ax_got.at[:, :, 4:, :], 1, axial=axial - 1)
-    soon_copy = remote(state_hbm.at[:, :, :4, :], ax_got.at[:, :, 4:, :], 1, axial=axial - 1)
-    right_copy = remote(sp_right, got_left, 2, span=span + 1)
-    left_copy = remote(sp_left, got_right, 3, span=span - 1)
-
-    when(odd, soon_copy.start)
-    coef_copy.start()
-    for copy in small_copies:
-        copy.start()
-
+    def axial_part(src, from_row, to_row, slot, part, target):
+        some = slice(*part)
+        return remote(
+            src.at[some, :, from_row : from_row + 4, :],
+            ax_got.at[some, :, to_row : to_row + 4, :],
+            slot,
+            axial=target,
+        )
+
+    down_copies, up_copies, soon_copies = [], [], []
+    for k, part in enumerate(parts):
+        down_copies.append(axial_part(u, rows - 4, 0, 2 * k, part, axial + 1))
+        up_copies.append(axial_part(u, 0, 4, 2 * k + 1, part, axial - 1))
+        soon_copies.append(axial_part(state_hbm, 0, 4, 2 * k + 1, part, axial - 1))
+    slots = 2 * len(parts)
+
+    def start_all(copies):
+        for copy in copies:
+            copy.start()
+
+    right_copy = remote(sp_right, got_left, slots, span=span + 1)
+    left_copy = remote(sp_left, got_right, slots + 1, span=span - 1)
+
+    when(odd, lambda: start_all(soon_copies))
+    if paired:
+        when(hub, lambda: tell(next_ready, axial=axial + 1, pitch=pitch - 1))
+    when(hub, lambda: tell(next_ready, axial=axial + 1))
+    when(both(under_hub, first), lambda: tell(next_ready, axial=axial - 1))
+    when(has_left, lambda: tell(span_ready, span=span - 1))
+    for other in range(1, npitch):
+        when(other > pitch, lambda: tell(pitch_ready, pitch=jnp.int32(other)))
     row = lax.broadcasted_iota(jnp.int32, (8, 128), 0)
     lane = lax.broadcasted_iota(jnp.int32, (8, 128), 1)
     group, place = lane // 4, lane % 4
     low_rows = row < 4
 
-    for copy in state_copies:
-        copy.wait()
-    when(both(has_up, even), up_copy.start)
-    when(both(has_down, even, no(both(hub_block, first))), down_copy.start)
+    state_copy.wait()
+    when(both(even, has_up), lambda: start_all(up_copies))
+    when(both(has_down, even, no(both(hub_block, first))), lambda: start_all(down_copies))
 
     groups = sp_left.shape[1]
 
@@ -181,7 +194,9 @@
     for f in range(fields):
         pack_span(f, 0)
     when(has_left, left_copy.start)
-    when(both(has_right, last_even), right_copy.start)
+    coef_copy.start()
+    for copy in small_copies:
+        copy.start()
 
     def flux_tile(t, carry):
         at = pl.ds(pl.multiple_of(t * 8, 8), 8)
@@ -217,7 +232,7 @@
     lax.fori_loop(0, tiles, flux_tile, 0, unroll=True)
 
     sum_copies = [
-        remote(sums, got_sums.at[step - 1], 3 + step, pitch=lax.rem(pitch + step, npitch))
+        remote(sums, got_sums.at[step - 1], slots + 1 + step, pitch=lax.rem(pitch + step, npitch))
         for step in range(1, npitch)
     ]
     when(pitch > 0, lambda: pl.semaphore_wait(pitch_ready, pitch))
@@ -248,21 +263,15 @@
             ax_own[f, i] = -pltpu.roll(ends, 4, 0)
         return carry
 
+    @pl.when(jnp.logical_or(under_hub, both(hub_block, first)))
+    def _():
+        pl.semaphore_wait(next_ready, 1)
+        start_all(down_copies)
+
     damp_field(0, 0)
-
-    @pl.when(under_hub)
-    def _():
-        pl.semaphore_wait(odd_ready, 1)
-        down_copy.start()
-
-    @pl.when(both(hub_block, first))
-    def _():
-        pl.semaphore_wait(even_ready, 1)
-        down_copy.start()
-
     damp_field(1, 0)
 
-    @pl.when(both(has_right, no(last_even)))
+    @pl.when(has_right)
     def _():
         pl.semaphore_wait(span_ready, 1)
         right_copy.start()
@@ -352,8 +361,6 @@
 
     lax.fori_loop(0, fields, carry_field, 0, unroll=True)
 
-    when(has_left, right_copy.wait_recv)
-    when(has_right, left_copy.wait_recv)
     outer = jnp.logical_or(lane < 4, lane >= 124)
     from_left = [jnp.where(place + t < 4, EDGE[t] * weight, 0.0) for t in range(4)]
     from_right = [jnp.where(place >= t, EDGE[t] * weight, 0.0) for t in range(4)]
@@ -378,10 +385,14 @@
                 out_ref[f, i, t * 8 : t * 8 + 8, :] += jnp.where(outer, moved, 0.0)
         return carry
 
-    lax.fori_loop(0, fields, span_field, 0, unroll=True)
-
-    when(has_up, down_copy.wait_recv)
-    when(has_down, up_copy.wait_recv)
+    def span_ends():
+        when(has_left, right_copy.wait_recv)
+        when(has_right, left_copy.wait_recv)
+        lax.fori_loop(0, fields, span_field, 0, unroll=True)
+
+    corner = both(axial == 0, span == 0)
+    when(no(corner), span_ends)
+
     near_low = [jnp.where(row + t < 4, EDGE[t] * weight, 0.0) for t in range(1, 4)]
     near_high = [jnp.where(row >= 4 + t, EDGE[t] * weight, 0.0) for t in range(1, 4)]
 
@@ -396,12 +407,18 @@
             out_ref[f, i, rows - 8 :, :] += jnp.where(low_rows, 0.0, ends)
         return carry
 
-    lax.fori_loop(0, fields, axial_field, 0, unroll=True)
+    for k, part in enumerate(parts):
+        when(has_up, down_copies[k].wait_recv)
+        when(has_down, up_copies[k].wait_recv)
+        for f in range(*part):
+            axial_field(f, 0)
+    when(corner, span_ends)
 
     for copy in sum_copies:
         copy.wait_send()
-    when(has_down, down_copy.wait_send)
-    when(has_up, up_copy.wait_send)
+    for k in range(len(parts)):
+        when(has_down, down_copies[k].wait_send)
+        when(has_up, up_copies[k].wait_send)
     when(has_right, right_copy.wait_send)
     when(has_left, left_copy.wait_send)
 
@@ -413,7 +430,7 @@
     vmem = lambda *shape: pltpu.VMEM(shape, jnp.float32)
     halo = (fields, cells, 8, lanes)
     packed = (fields, groups, 8, lanes)
-    sems = 4 + npitch - 1
+    sems = 2 * len(split(fields)) + 2 + npitch - 1
     return pl.pallas_call(
         functools.partial(kernel, sizes),
         out_shape=pltpu.VMEM(state.shape, jnp.float32),
@@ -442,8 +459,7 @@
             pltpu.SemaphoreType.REGULAR,
             pltpu.SemaphoreType.REGULAR,
             pltpu.SemaphoreType.REGULAR,
-            pltpu.SemaphoreType.REGULAR,
-            pltpu.SemaphoreType.DMA((3 + fields,)),
+            pltpu.SemaphoreType.DMA((4,)),
             pltpu.SemaphoreType.DMA((sems,)),
             pltpu.SemaphoreType.DMA((sems,)),
         ],

time: 8.68 us -> 8.53 us (0.983)
  Pallas kernels: 7.02 us -> 6.87 us
    pallas_call x1, Pallas kernels: 7.02 us -> 6.87 us  [shards(): pl.pallas_call(functools.partial(kernel, sizes), out_shape=pltpu.VMEM(sta...]
where the time goes in v3:
time: 8.53 us; the launch traced here: 8.37 us
  Pallas kernels  6.87 us (81%)
  local copies, waits for them, and re-layouts  0.84 us (10%)
  between operations  0.66 us (8%)
    pallas_call x1, Pallas kernels, shards(): pl.pallas_call(functools.partial(kernel, sizes), out_shape=pltpu.VMEM(sta...  6.87 us
    unnamed x1, local copies, waits for them, and re-layouts  0.84 us

profile of v3, /device:TPU:0, one launch (start us, length us, event | category | flops | bytes accessed | tf_op | source)
XLA Modules:
  0.0 8.4 jit_solution(8380289692889998820)
XLA Ops:
  0.7 6.9 %shard_map.46 = f32[5,8,32,128]{3,2,1,0:T(8,128)S(1)} custom-call(s32[1]{0:T(128)S(6)} %copy.7.lag_hbm, s32[1,128]{1,0:T(1,128)} %bitcast.1, f32[5,8,32,128]{3,2,1,0:T(8,128)} %state_hbm.1, f32[2,4,5,32,128]{4,3,2,1,0:T(8,128)} %coef_hbm.1), custom_call_target="tpu_custom_call" | custom-call | tf_op jit(solution)/shard_map/pallas_call | solution.py:434
  7.5 0.8 %copy.6 = f32[5,8,32,128]{3,2,1,0:T(8,128)} copy(f32[5,8,32,128]{3,2,1,0:T(8,128)S(1)} %shard_map.46) | data formatting | bytes 1310720

commit v4 on v3

--- a/solution.py
+++ b/solution.py
@@ -14,6 +14,7 @@
 DAMPING = 0.5
 EDGE = (1.0, -8.0, 28.0, -56.0)
 MESH = pl.DeviceIdType.MESH
+AXIAL_CUTS, SPAN_CUTS = (4,), (3,)
 
 
 def line_root(main, side):
@@ -21,8 +22,8 @@
     return root, 1.0 / (main + 2.0 * side * root)
 
 
-def split(fields):
-    cuts = sorted({0, fields * 2 // 5, fields * 4 // 5, fields})
+def split(fields, *fifths):
+    cuts = sorted({0, *(fields * n // 5 for n in fifths), fields})
     return tuple(zip(cuts[:-1], cuts[1:]))
 
 
@@ -64,7 +65,7 @@
     npitch, naxial, nspan = sizes
     fields, cells, rows, _ = u.shape
     tiles = rows // 8
-    parts = split(fields)
+    parts, span_parts = split(fields, *AXIAL_CUTS), split(fields, *SPAN_CUTS)
     harm_max = co.shape[1]
     total = cells * npitch
     diffusion = float(total * total // 64)
@@ -72,12 +73,13 @@
     q, q_scale = line_root(1.0 + 2.0 * diffusion, -diffusion)
     pitch, axial, span = (lax.axis_index(name) for name in ("pitch", "axial", "span"))
 
-    state_copy = pltpu.make_async_copy(state_hbm, u, local_sem.at[3])
+    state_copies = [
+        pltpu.make_async_copy(state_hbm.at[f], u.at[f], local_sem.at[0]) for f in range(fields)
+    ]
+    state_copy = pltpu.make_async_copy(state_hbm, u, local_sem.at[0])
     coef_copy = pltpu.make_async_copy(coef_hbm, co, local_sem.at[0])
-    small_copies = [
-        pltpu.make_async_copy(lag_hbm, lag_ref, local_sem.at[1]),
-        pltpu.make_async_copy(harm_hbm, harm_ref, local_sem.at[2]),
-    ]
+    lag_copy = pltpu.make_async_copy(lag_hbm, lag_ref, local_sem.at[1])
+    harm_copy = pltpu.make_async_copy(harm_hbm, harm_ref, local_sem.at[1])
 
     def when(flag, action):
         @pl.when(flag)
@@ -90,7 +92,7 @@
     def no(flag):
         return jnp.logical_not(flag)
 
-    paired = npitch % 2 == 0
+    paired = npitch % 2 == 0 and naxial % 2 == 0
     has_up, has_down = axial > 0, axial < naxial - 1
     has_left, has_right = span > 0, span < nspan - 1
     odd = lax.rem(axial, 2) == 1
@@ -100,9 +102,12 @@
     second = lax.rem(pitch, 2) == 1 if paired else pitch >= 0
     first = no(second)
     hub = both(hub_block, second)
+    far_hub = both(odd, second, axial > 2)
     under_hub = both(odd, has_down)
 
-    state_copy.start()
+    for copy in state_copies:
+        copy.start()
+    lag_copy.start()
     barrier = pltpu.get_barrier_semaphore()
 
     def tell(semaphore, **where):
@@ -111,58 +116,68 @@
     def count(*flags):
         return sum(jnp.where(flag, 1, 0) for flag in flags)
 
-    heard_by = pitch
+    told_axial, told_pitch = jnp.where(odd, axial - 1, axial - 2), pitch
     if paired:
-        heard_by = jnp.where(both(first, jnp.logical_or(even, has_down)), pitch + 1, pitch)
-    when(
-        has_up,
-        lambda: tell(barrier, axial=jnp.where(odd, axial - 1, axial - 2), pitch=heard_by),
-    )
+        told_axial = jnp.where(both(first, even), axial + 1, told_axial)
+        told_axial = jnp.where(both(first, under_hub), axial + 2, told_axial)
+        told_pitch = jnp.where(both(first, jnp.logical_or(even, has_down)), pitch + 1, pitch)
+    when(has_up, lambda: tell(barrier, axial=told_axial, pitch=told_pitch))
     when(has_down, lambda: tell(barrier, axial=axial + 1))
     when(has_right, lambda: tell(barrier, span=span + 1))
     for other in range(npitch - 1):
         when(other < pitch, lambda: tell(barrier, pitch=jnp.int32(other)))
 
     heard = count(has_left, has_up, both(last_even, has_down))
-    heard = heard + count(hub, hub) * (2 if paired else 1) + (npitch - 1 - pitch)
+    heard = heard + 2 * count(hub) + (npitch - 1 - pitch)
+    if paired:
+        heard = heard + 2 * count(far_hub)
     pl.semaphore_wait(barrier, heard)
 
-    def remote(src, dst, slot, **where):
+    def remote(src, dst, sent, got, **where):
         return pltpu.make_async_remote_copy(
             src_ref=src,
             dst_ref=dst,
-            send_sem=send_sem.at[slot],
-            recv_sem=recv_sem.at[slot],
+            send_sem=send_sem.at[sent],
+            recv_sem=recv_sem.at[got],
             device_id=where,
             device_id_type=MESH,
         )
 
-    def axial_part(src, from_row, to_row, slot, part, target):
-        some = slice(*part)
+    def axial_part(src, from_row, to_row, sent, got, some, target):
         return remote(
             src.at[some, :, from_row : from_row + 4, :],
             ax_got.at[some, :, to_row : to_row + 4, :],
-            slot,
+            sent,
+            got,
             axial=target,
         )
 
     down_copies, up_copies, soon_copies = [], [], []
     for k, part in enumerate(parts):
-        down_copies.append(axial_part(u, rows - 4, 0, 2 * k, part, axial + 1))
-        up_copies.append(axial_part(u, 0, 4, 2 * k + 1, part, axial - 1))
-        soon_copies.append(axial_part(state_hbm, 0, 4, 2 * k + 1, part, axial - 1))
+        some = slice(*part)
+        down_copies.append(axial_part(u, rows - 4, 0, 0, 2 * k, some, axial + 1))
+        up_copies.append(axial_part(u, 0, 4, 1, 2 * k + 1, some, axial - 1))
+        soon_copies.append(axial_part(state_hbm, 0, 4, 1, 2 * k + 1, some, axial - 1))
+    down_sent = axial_part(u, rows - 4, 0, 0, 0, slice(0, fields), axial + 1)
+    up_sent = axial_part(u, 0, 4, 1, 1, slice(0, fields), axial - 1)
     slots = 2 * len(parts)
+    right_copy = remote(sp_right, got_left, 2, slots, span=span + 1)
+    left_copies = []
+    for k, part in enumerate(span_parts):
+        some = slice(*part)
+        left_copies.append(
+            remote(sp_left.at[some], got_right.at[some], 3, slots + 1 + k, span=span - 1)
+        )
+    left_sent = remote(sp_left, got_right, 3, slots + 1, span=span - 1)
+    slots = slots + 1 + len(span_parts)
 
     def start_all(copies):
         for copy in copies:
             copy.start()
 
-    right_copy = remote(sp_right, got_left, slots, span=span + 1)
-    left_copy = remote(sp_left, got_right, slots + 1, span=span - 1)
-
     when(odd, lambda: start_all(soon_copies))
     if paired:
-        when(hub, lambda: tell(next_ready, axial=axial + 1, pitch=pitch - 1))
+        when(far_hub, lambda: tell(next_ready, axial=axial - 2, pitch=pitch - 1))
     when(hub, lambda: tell(next_ready, axial=axial + 1))
     when(both(under_hub, first), lambda: tell(next_ready, axial=axial - 1))
     when(has_left, lambda: tell(span_ready, span=span - 1))
@@ -191,12 +206,13 @@
             sp_left[f, g] = left
         return carry
 
-    for f in range(fields):
-        pack_span(f, 0)
-    when(has_left, left_copy.start)
+    for k, part in enumerate(span_parts):
+        for f in range(*part):
+            pack_span(f, 0)
+        when(has_left, left_copies[k].start)
     coef_copy.start()
-    for copy in small_copies:
-        copy.start()
+    lag_copy.wait()
+    harm_copy.start()
 
     def flux_tile(t, carry):
         at = pl.ds(pl.multiple_of(t * 8, 8), 8)
@@ -232,7 +248,7 @@
     lax.fori_loop(0, tiles, flux_tile, 0, unroll=True)
 
     sum_copies = [
-        remote(sums, got_sums.at[step - 1], slots + 1 + step, pitch=lax.rem(pitch + step, npitch))
+        remote(sums, got_sums.at[step - 1], 3 + step, slots - 1 + step, pitch=lax.rem(pitch + step, npitch))
         for step in range(1, npitch)
     ]
     when(pitch > 0, lambda: pl.semaphore_wait(pitch_ready, pitch))
@@ -279,8 +295,7 @@
     for f in range(2, fields):
         damp_field(f, 0)
 
-    for copy in small_copies:
-        copy.wait()
+    harm_copy.wait()
     order = row.astype(jnp.float32) + 1.0
     phase = (2.0 * math.pi / PERIOD_SAMPLES) * order * lag_ref[0].astype(jnp.float32)
     active = row < harm_ref[...]
@@ -387,8 +402,10 @@
 
     def span_ends():
         when(has_left, right_copy.wait_recv)
-        when(has_right, left_copy.wait_recv)
-        lax.fori_loop(0, fields, span_field, 0, unroll=True)
+        for k, part in enumerate(span_parts):
+            when(has_right, left_copies[k].wait_recv)
+            for f in range(*part):
+                span_field(f, 0)
 
     corner = both(axial == 0, span == 0)
     when(no(corner), span_ends)
@@ -416,11 +433,10 @@
 
     for copy in sum_copies:
         copy.wait_send()
-    for k in range(len(parts)):
-        when(has_down, down_copies[k].wait_send)
-        when(has_up, up_copies[k].wait_send)
+    when(has_down, down_sent.wait_send)
+    when(has_up, up_sent.wait_send)
     when(has_right, right_copy.wait_send)
-    when(has_left, left_copy.wait_send)
+    when(has_left, left_sent.wait_send)
 
 
 def shards(sizes, state, coeffs, lag_shift, harmonics):
@@ -430,7 +446,7 @@
     vmem = lambda *shape: pltpu.VMEM(shape, jnp.float32)
     halo = (fields, cells, 8, lanes)
     packed = (fields, groups, 8, lanes)
-    sems = 2 * len(split(fields)) + 2 + npitch - 1
+    arrivals = 2 * len(split(fields, *AXIAL_CUTS)) + 1 + len(split(fields, *SPAN_CUTS)) + npitch - 1
     return pl.pallas_call(
         functools.partial(kernel, sizes),
         out_shape=pltpu.VMEM(state.shape, jnp.float32),
@@ -459,9 +475,9 @@
             pltpu.SemaphoreType.REGULAR,
             pltpu.SemaphoreType.REGULAR,
             pltpu.SemaphoreType.REGULAR,
-            pltpu.SemaphoreType.DMA((4,)),
-            pltpu.SemaphoreType.DMA((sems,)),
-            pltpu.SemaphoreType.DMA((sems,)),
+            pltpu.SemaphoreType.DMA((2,)),
+            pltpu.SemaphoreType.DMA((4 + npitch - 1,)),
+            pltpu.SemaphoreType.DMA((arrivals,)),
         ],
         compiler_params=pltpu.CompilerParams(collective_id=0, has_side_effects=True),
     )(lag_shift, harmonics.reshape(1, lanes), state, coeffs)

time: 8.53 us -> 8.48 us (level)
  no operation moved by 1% of the time
where the time goes in v4:
time: 8.48 us; the launch traced here: 8.32 us
  Pallas kernels  6.83 us (81%)
  local copies, waits for them, and re-layouts  0.84 us (10%)
  between operations  0.66 us (8%)
    pallas_call x1, Pallas kernels, shards(): pl.pallas_call(functools.partial(kernel, sizes), out_shape=pltpu.VMEM(sta...  6.83 us
    unnamed x1, local copies, waits for them, and re-layouts  0.84 us

profile of v4, /device:TPU:0, one launch (start us, length us, event | category | flops | bytes accessed | tf_op | source)
XLA Modules:
  0.0 8.3 jit_solution(8668149059149432695)
XLA Ops:
  0.7 6.8 %shard_map.46 = f32[5,8,32,128]{3,2,1,0:T(8,128)S(1)} custom-call(s32[1]{0:T(128)S(6)} %copy.7.lag_hbm, s32[1,128]{1,0:T(1,128)} %bitcast.1, f32[5,8,32,128]{3,2,1,0:T(8,128)} %state_hbm.1, f32[2,4,5,32,128]{4,3,2,1,0:T(8,128)} %coef_hbm.1), custom_call_target="tpu_custom_call" | custom-call | tf_op jit(solution)/shard_map/pallas_call | solution.py:450
  7.5 0.8 %copy.6 = f32[5,8,32,128]{3,2,1,0:T(8,128)} copy(f32[5,8,32,128]{3,2,1,0:T(8,128)S(1)} %shard_map.46) | data formatting | bytes 1310720

commit v5 on v4

--- a/solution.py
+++ b/solution.py
@@ -73,10 +73,14 @@
     q, q_scale = line_root(1.0 + 2.0 * diffusion, -diffusion)
     pitch, axial, span = (lax.axis_index(name) for name in ("pitch", "axial", "span"))
 
-    state_copies = [
-        pltpu.make_async_copy(state_hbm.at[f], u.at[f], local_sem.at[0]) for f in range(fields)
-    ]
-    state_copy = pltpu.make_async_copy(state_hbm, u, local_sem.at[0])
+    state_copies, part_copies = [], []
+    for k, part in enumerate(span_parts):
+        some = slice(*part)
+        part_copies.append(pltpu.make_async_copy(state_hbm.at[some], u.at[some], local_sem.at[k]))
+        for f in range(*part):
+            state_copies.append(
+                pltpu.make_async_copy(state_hbm.at[f], u.at[f], local_sem.at[k])
+            )
     coef_copy = pltpu.make_async_copy(coef_hbm, co, local_sem.at[0])
     lag_copy = pltpu.make_async_copy(lag_hbm, lag_ref, local_sem.at[1])
     harm_copy = pltpu.make_async_copy(harm_hbm, harm_ref, local_sem.at[1])
@@ -107,7 +111,6 @@
 
     for copy in state_copies:
         copy.start()
-    lag_copy.start()
     barrier = pltpu.get_barrier_semaphore()
 
     def tell(semaphore, **where):
@@ -175,7 +178,9 @@
         for copy in copies:
             copy.start()
 
-    when(odd, lambda: start_all(soon_copies))
+    held = both(under_hub, first, has_left)
+    when(odd, lambda: start_all(soon_copies[:-1]))
+    when(both(odd, no(held)), soon_copies[-1].start)
     if paired:
         when(far_hub, lambda: tell(next_ready, axial=axial - 2, pitch=pitch - 1))
     when(hub, lambda: tell(next_ready, axial=axial + 1))
@@ -188,9 +193,14 @@
     group, place = lane // 4, lane % 4
     low_rows = row < 4
 
-    state_copy.wait()
-    when(both(even, has_up), lambda: start_all(up_copies))
-    when(both(has_down, even, no(both(hub_block, first))), lambda: start_all(down_copies))
+    late = both(even, no(both(hub_block, first)))
+
+    @pl.when(late)
+    def _():
+        for copy in part_copies:
+            copy.wait()
+        when(has_up, lambda: start_all(up_copies))
+        when(has_down, lambda: start_all(down_copies))
 
     groups = sp_left.shape[1]
 
@@ -207,12 +217,20 @@
         return carry
 
     for k, part in enumerate(span_parts):
+        when(no(late), part_copies[k].wait)
         for f in range(*part):
             pack_span(f, 0)
         when(has_left, left_copies[k].start)
+    when(both(even, has_up, no(late)), lambda: start_all(up_copies))
     coef_copy.start()
-    lag_copy.wait()
-    harm_copy.start()
+    lag_copy.start()
+
+    ahead = both(under_hub, second, has_left)
+
+    @pl.when(ahead)
+    def _():
+        pl.semaphore_wait(next_ready, 1)
+        start_all(down_copies)
 
     def flux_tile(t, carry):
         at = pl.ds(pl.multiple_of(t * 8, 8), 8)
@@ -279,10 +297,14 @@
             ax_own[f, i] = -pltpu.roll(ends, 4, 0)
         return carry
 
-    @pl.when(jnp.logical_or(under_hub, both(hub_block, first)))
+    @pl.when(jnp.logical_or(both(under_hub, no(ahead)), both(hub_block, first)))
     def _():
         pl.semaphore_wait(next_ready, 1)
         start_all(down_copies)
+
+    when(held, soon_copies[-1].start)
+    lag_copy.wait()
+    harm_copy.start()
 
     damp_field(0, 0)
     damp_field(1, 0)
@@ -429,7 +451,8 @@
         when(has_down, up_copies[k].wait_recv)
         for f in range(*part):
             axial_field(f, 0)
-    when(corner, span_ends)
+        if k == 0:
+            when(corner, span_ends)
 
     for copy in sum_copies:
         copy.wait_send()

time: 8.48 us -> 8.38 us (0.988)
  Pallas kernels: 6.83 us -> 6.72 us
    pallas_call x1, Pallas kernels: 6.83 us -> 6.72 us  [shards(): pl.pallas_call(functools.partial(kernel, sizes), out_shape=pltpu.VMEM(sta...]
where the time goes in v5:
time: 8.38 us; the launch traced here: 8.22 us
  Pallas kernels  6.72 us (80%)
  local copies, waits for them, and re-layouts  0.84 us (10%)
  between operations  0.66 us (8%)
    pallas_call x1, Pallas kernels, shards(): pl.pallas_call(functools.partial(kernel, sizes), out_shape=pltpu.VMEM(sta...  6.72 us
    unnamed x1, local copies, waits for them, and re-layouts  0.84 us

profile of v5, /device:TPU:0, one launch (start us, length us, event | category | flops | bytes accessed | tf_op | source)
XLA Modules:
  0.0 8.2 jit_solution(12700267507494763311)
XLA Ops:
  0.7 6.7 %shard_map.46 = f32[5,8,32,128]{3,2,1,0:T(8,128)S(1)} custom-call(s32[1]{0:T(128)S(6)} %copy.7.lag_hbm, s32[1,128]{1,0:T(1,128)} %bitcast.1, f32[5,8,32,128]{3,2,1,0:T(8,128)} %state_hbm.1, f32[2,4,5,32,128]{4,3,2,1,0:T(8,128)} %coef_hbm.1), custom_call_target="tpu_custom_call" | custom-call | tf_op jit(solution)/shard_map/pallas_call | solution.py:473
  7.4 0.8 %copy.6 = f32[5,8,32,128]{3,2,1,0:T(8,128)} copy(f32[5,8,32,128]{3,2,1,0:T(8,128)S(1)} %shard_map.46) | data formatting | bytes 1310720
